TPU v7x, 32 devices: a whole 2x2x4 slice. The times are simulated.
32 devices in a mesh: row: 8 (over y, x, core), col: 4 (over z).
Axes of the slice: x: 2, y: 2, z: 4, core: 2. Of those that a mesh axis runs over, the one named last changes fastest.
Arguments:
- diag_blocks: float32 [16, 512, 512], P('row', None, 'col'), as said below
- near_blocks: float32 [16, 4, 512, 512], P('row', None, None, 'col'), may hold values from -0.1 to 0.1, as said below
- cluster_bases: float32 [16, 512, 512], P('row', 'col'), as said below
- near_ids: int32 [16, 4], P('row'), may hold values from 0 to 15, as said below
- near_count: int32 [16], P('row'), may hold values from 1 to 4
- parent_bases: float32 [8, 512, 512], P('row'), as said below
Outputs:
- leaf_diag: float32 [16, 256, 256], P('row', None, 'col')
- leaf_near: float32 [16, 4, 256, 256], P('row', None, None, 'col')
- parent_diag: float32 [8, 256, 256], P('row', None, 'col')
Inputs may be any that keep to these rules, and one draw needn't show every extreme that they name: `near_ids`: slot 0 of cluster i names its sibling: i + 2 when i // 2 is even, else i - 2. The other slots may name any cluster. For sibling clusters a and b = a + 2 (a // 2 even), near_blocks[b, 0] is the transpose of near_blocks[a, 0]. `diag_blocks`: Symmetric. `cluster_bases`: the identity plus a small full-rank perturbation. `parent_bases`: the identity plus a small full-rank perturbation.
All inputs are finite; a program needn't handle non-finite values.
Results may differ from a plain program's by a relative error of at most 0.0003.
Values sent between devices are 32-bit elements; how exact they have to be, the bound alone decides.
No kernel may reach another device: no remote copies, remote signals or barrier semaphores. Data moves between devices by JAX's collectives and lax.ppermute only.
A program may use at most 128 MiB of HBM per device.

v0:
```python
import jax
import jax.numpy as jnp
from jax import lax
from jax.sharding import PartitionSpec as P

B = 512
K = 256
NEAR = 4
highest = lax.Precision.HIGHEST


def partner(shard, axis, apart):
    return lax.ppermute(shard, axis, [(i, i ^ 1 << apart) for i in range(lax.axis_size(axis))])


def eliminate(dense, redundant):
    factor = jnp.linalg.cholesky(dense[:redundant, :redundant])
    solved = jax.scipy.linalg.cho_solve((factor, True), dense[:redundant, redundant:])
    schur = dense[redundant:, redundant:] - jnp.dot(
        dense[redundant:, :redundant], solved, precision=highest
    )
    return (solved, schur)


def per_device(diag_blocks, near_blocks, cluster_bases, near_ids, near_count, parent_bases):
    clusters = diag_blocks.shape[0]
    redundant = B - K
    column = lax.axis_index("col")
    quarter = K // lax.axis_size("col")
    own_rows = cluster_bases.shape[1]
    full_bases = lax.all_gather(cluster_bases, "col", axis=1, tiled=True)
    partial_value = jnp.einsum("cij,cjk->cik", diag_blocks, cluster_bases, precision=highest)
    summed = lax.psum(partial_value, "col")
    dense = jnp.einsum("cji,cjk->cik", full_bases, summed, precision=highest)
    solved, schur = jax.vmap(lambda single: eliminate(single, redundant))(dense)
    leaf_diag = lax.dynamic_slice_in_dim(schur, column * quarter, quarter, 2)
    flat_ids = near_ids.reshape(-1)
    shards = lax.all_gather(cluster_bases[:, :, redundant:], "row", axis=0, tiled=True)
    number = shards.shape[0]
    one_hot = (flat_ids[:, None] == jnp.arange(number, dtype=jnp.int32)[None, :]).astype(
        jnp.float32
    )
    picked = jnp.dot(one_hot, shards.reshape(number, -1), precision=highest)
    picked = picked.reshape(clusters, NEAR, own_rows, K)
    terms = jnp.einsum("cnij,cnjk->cnik", near_blocks, picked, precision=highest)
    right_part = lax.psum_scatter(terms, "col", scatter_dimension=3, tiled=True)
    moved = jnp.einsum("cji,cnjk->cnik", full_bases, right_part, precision=highest)
    coupled = moved[:, :, redundant:, :] - jnp.einsum(
        "cri,cnrk->cnik", solved, moved[:, :, :redundant, :], precision=highest
    )
    live = (jnp.arange(NEAR, dtype=jnp.int32)[None, :] < near_count[:, None]).astype(jnp.float32)
    leaf_near = coupled * live[:, :, None, None]
    halfway = clusters // 2
    parity = lax.axis_index("row") % 2
    stacked = jnp.stack([leaf_diag, leaf_near[:, 0]])
    kept = lax.dynamic_slice_in_dim(stacked, parity * halfway, halfway, 1)
    outgoing = lax.dynamic_slice_in_dim(stacked, (1 - parity) * halfway, halfway, 1)
    arrived = partner(outgoing, "row", 0)
    first_child = jnp.where(parity == 0, kept, arrived)
    second_child = jnp.where(parity == 0, arrived, kept)
    left_columns = jnp.concatenate([first_child[0], second_child[1]], axis=1)
    right_columns = jnp.concatenate([first_child[1], second_child[0]], axis=1)
    merged = jnp.concatenate([left_columns, right_columns], axis=2)
    rows_first = lax.dynamic_slice_in_dim(parent_bases, column * quarter, quarter, 1)
    rows_second = lax.dynamic_slice_in_dim(parent_bases, K + column * quarter, quarter, 1)
    chosen_rows = jnp.concatenate([rows_first, rows_second], axis=1)
    lifted = jnp.einsum("hji,hjk->hik", parent_bases, merged, precision=highest)
    parent_part = jnp.einsum("hij,hjk->hik", lifted, chosen_rows, precision=highest)
    parent_dense = lax.psum(parent_part, "col")
    parent_schur = jax.vmap(lambda single: eliminate(single, K)[1])(parent_dense)
    parent_diag = lax.dynamic_slice_in_dim(parent_schur, column * quarter, quarter, 2)
    return (leaf_diag, leaf_near, parent_diag)


def solution(mesh):
    return jax.shard_map(
        per_device,
        mesh=mesh,
        in_specs=(
            P("row", None, "col"),
            P("row", None, None, "col"),
            P("row", "col", None),
            P("row", None),
            P("row"),
            P("row", None, None),
        ),
        out_specs=(P("row", None, "col"), P("row", None, None, "col"), P("row", None, "col")),
        check_vma=False,
    )
```

profile of v0, /device:TPU:0, one launch (start us, length us, event | category | flops | bytes accessed | tf_op | source)
XLA Modules:
  0.0 401.4 jit_solution(10855884119777863552)
XLA Ops:
  8.1 1.8 slice.175
  9.9 4.4 %fusion.60 = f32[2,512,512]{2,1,0:T(8,128)} fusion(f32[2,512,128]{2,1,0:T(8,128)} %param.6, f32[2,128,512]{2,1,0:T(8,128)} %param.8), kind=kOutput, calls=%fused_computation.129 | convolution fusion | flops 805306368 | bytes 3145728 | tf_op jit(solution)/shard_map/cij,cjk->cik/dot_general | solution.py:32
  15.1 26.7 %all-gather.5.cloned.1.call-done = f32[16,128,256]{2,1,0:T(8,128)} async-done(((f32[2,128,256]{2,1,0:T(8,128)}), f32[16,128,256]{2,1,0:T(8,128)}) %all-gather.5.cloned.1.call-update) | async-done | bytes 2097168 | tf_op jit(solution)/shard_map/all_gather | solution.py:38
  41.8 3.8 fusion
  45.7 5.1 %convolution_bitcast_fusion = f32[2,4,512,256]{2,3,1,0:T(8,128)} fusion(f32[2,4,512,128]{3,2,1,0:T(8,128)S(1)} %copy-done, f32[2,4,128,256]{3,1,2,0:T(4,128)S(1)} %fusion), kind=kOutput, calls=%fused_computation.4 | convolution fusion | flops 1610612736 | bytes 7340032 | tf_op jit(solution)/shard_map/cnij,cnjk->cnik/dot_general | solution.py:45
  51.5 75.6 %all-reduce.5.cloned.1.call-done = f32[2,512,512]{2,1,0:T(8,128)} async-done(((f32[2,512,512]{2,1,0:T(8,128)}), f32[2,512,512]{2,1,0:T(8,128)}) %all-reduce.5.cloned.1.call-update) | async-done | bytes 2097168 | tf_op jit(solution)/shard_map/psum | solution.py:33
  127.1 5.7 %convolution_bitcast_fusion.1 = f32[2,512,512]{1,2,0:T(8,128)S(1)} fusion(f32[2,512,512]{2,1,0:T(8,128)} %all-reduce.5.cloned.1.call-done, f32[2,512,512]{2,1,0:T(8,128)} %all-gather.3.cloned.1.call-done), kind=kOutput, calls=%fused_computation.10 | convolution fusion | flops 3221225472 | bytes 6291456 | tf_op jit(solution)/shard_map/cji,cjk->cik/dot_general | solution.py:34
  132.8 1.3 copy-done.1
  137.3 23.9 %custom-call.40 = f32[2,128,128]{2,1,0:T(8,128)S(1)} custom-call(f32[2,128,128]{2,1,0:T(8,128)S(1)} %cholesky.239), custom_call_target="Cholesky" | custom-call | tf_op jit(solution)/shard_map/vmap(jit(cholesky))/cholesky | solution.py:17
  161.3 19.7 %custom-call.41 = f32[2,1,128,128]{2,3,1,0:T(8,128)S(1)} custom-call(f32[2,1,128,128]{3,2,1,0:T(8,128)S(1)} %select_bitcast_fusion), custom_call_target="InvertDiagBlocksLowerTriangular" | custom-call | tf_op jit(solution)/shard_map/vmap(jit(cholesky))/cholesky | solution.py:17
  180.9 1.2 constant_dynamic-update-slice_fusion.2
  182.1 1.3 convolution_subtract_fusion.3
  183.4 23.5 %custom-call.42 = f32[2,128,128]{2,1,0:T(8,128)S(1)} custom-call(f32[2,128,128]{2,1,0:T(8,128)S(1)} %convolution_subtract_fusion.3), custom_call_target="Cholesky" | custom-call | tf_op jit(solution)/shard_map/vmap(jit(cholesky))/cholesky | solution.py:17
  207.3 3.9 while.2
  208.0 1.3 bitcast_dynamic-update-slice_fusion.5
  209.9 1.3 bitcast_dynamic-update-slice_fusion.5
  211.2 39.5 %custom-call.43 = f32[2,2,128,128]{2,3,1,0:T(8,128)S(1)} custom-call(f32[2,2,128,128]{3,2,1,0:T(8,128)S(1)} %bitcast.192), custom_call_target="InvertDiagBlocksLowerTriangular" | custom-call | tf_op jit(solution)/shard_map/vmap(jit(_cho_solve))/triangular_solve | solution.py:18
  250.7 1.4 fusion.20
  252.1 1.6 convolution_subtract_fusion.1
  255.3 2.1 fusion.16
  258.4 3.9 fusion.4
  267.0 2.0 convolution_bitcast_fusion.2
  269.1 51.3 %all-reduce.7.cloned.1.call-done = f32[1,512,512]{1,2,0:T(8,128)} async-done(((f32[1,512,512]{1,2,0:T(8,128)}), f32[1,512,512]{1,2,0:T(8,128)}) %all-reduce.7.cloned.1.call-update) | async-done | bytes 1048592 | tf_op jit(solution)/shard_map/psum | solution.py:69
  320.4 1.9 fusion.59
  325.2 11.7 %custom-call.44 = f32[1,128,128]{2,1,0:T(8,128)S(1)} custom-call(f32[1,128,128]{2,1,0:T(8,128)S(1)} %cholesky.242), custom_call_target="Cholesky" | custom-call | tf_op jit(solution)/shard_map/vmap(jit(cholesky))/cholesky | solution.py:17
  337.0 10.0 %custom-call.45 = f32[1,1,128,128]{2,3,1,0:T(8,128)S(1)} custom-call(f32[1,1,128,128]{3,2,1,0:T(8,128)S(1)} %get-tuple-element.57), custom_call_target="InvertDiagBlocksLowerTriangular" | custom-call | tf_op jit(solution)/shard_map/vmap(jit(cholesky))/cholesky | solution.py:17
  349.1 11.7 %custom-call.46 = f32[1,128,128]{2,1,0:T(8,128)S(1)} custom-call(f32[1,128,128]{2,1,0:T(8,128)S(1)} %fusion.11), custom_call_target="Cholesky" | custom-call | tf_op jit(solution)/shard_map/vmap(jit(cholesky))/cholesky | solution.py:17
  364.3 5.3 %while.3 = (s32[]{:T(128)}, f32[1,256,256]{2,1,0:T(8,128)S(1)}, s32[2,2]{1,0:T(2,128)S(1)}, f32[2,1,128,128]{3,2,1,0:T(8,128)}, s32[]{:T(128)}) while((s32[]{:T(128)}, f32[1,256,256]{2,1,0:T(8,128)S(1)}, s32[2,2]{1,0:T(2,128)S(1)}, f32[2,1,128,128]{3,2,1,0:T(8,128)}, s32[]{:T(128)}) %tuple.66), condition=%wide.while_cond.1, body=%wide.while_body.1.sunk | while | flops 2 | bytes 132205 | solution.py:18
  365.0 2.0 bitcast_dynamic-update-slice_fusion.6
  367.6 2.0 bitcast_dynamic-update-slice_fusion.6
  369.6 20.5 %custom-call.47 = f32[1,2,128,128]{2,3,1,0:T(8,128)S(1)} custom-call(f32[1,2,128,128]{3,2,1,0:T(8,128)} %bitcast.193), custom_call_target="InvertDiagBlocksLowerTriangular" | custom-call | tf_op jit(solution)/shard_map/vmap(jit(_cho_solve))/triangular_solve | solution.py:18
  392.6 1.5 dynamic-slice_subtract_fusion.1
  (92 shorter events, 24.7 us)
Async XLA Ops:
  8.0 37.7 %copy-start = (f32[2,4,512,128]{3,2,1,0:T(8,128)S(1)}, f32[2,4,512,128]{3,2,1,0:T(8,128)}, u32[]{:S(2)}) copy-start(f32[2,4,512,128]{3,2,1,0:T(8,128)} %param.7) | copy-start | bytes 6291460
  8.0 33.8 %all-gather.5.cloned.1.call-start = ((), (), s32[]{:S(2)}) async-start(), calls=%async_computation.3 | async-start | bytes 2359296 | tf_op jit(solution)/shard_map/all_gather | solution.py:38
  9.9 117.2 %all-reduce.5.cloned.1.call-start = ((), (), s32[]{:S(2)}) async-start(), calls=%async_computation.1 | async-start | bytes 4194304 | tf_op jit(solution)/shard_map/psum | solution.py:33
  14.3 27.5 %copy-start.9 = (s32[2,4]{1,0:T(2,128)S(1)}, s32[2,4]{1,0:T(2,128)}, u32[]{:S(2)}) copy-start(s32[2,4]{1,0:T(2,128)} %param.9) | copy-start | bytes 100
  14.3 112.8 %all-gather.3.cloned.1.call-start = ((), (), s32[]{:S(2)}) async-start(), calls=%async_computation.2 | async-start | bytes 2621440 | tf_op jit(solution)/shard_map/all_gather | solution.py:31
  15.1 243.3 %reduce-scatter.2.cloned.1.call-start = ((), (), s32[]{:S(2)}) async-start(), calls=%async_computation.4 | async-start | bytes 5242880 | tf_op jit(solution)/shard_map/reduce_scatter | solution.py:46
  50.8 0.7 copy-start.10
  50.8 269.6 %all-reduce.7.cloned.1.call-start = ((), (), s32[]{:S(2)}) async-start(), calls=%async_computation.5 | async-start | bytes 2097152 | tf_op jit(solution)/shard_map/psum | solution.py:69
  132.8 1.3 copy-start.1
  136.4 0.8 copy-start.4
  258.3 7.0 %copy-start.5 = (f32[2,256,64]{1,2,0:T(8,128)}, f32[2,256,64]{1,2,0:T(8,128)S(1)}, u32[]{:S(2)}) copy-start(f32[2,256,64]{1,2,0:T(8,128)S(1)} %dynamic-slice_subtract_fusion) | copy-start | bytes 393220
  262.9 0.8 copy-start.7
  263.7 2.6 copy-start.3
  263.8 1.5 collective-permute-start
  322.3 67.8 %copy-start.2 = (f32[1,512,512]{1,2,0:T(8,128)S(1)}, f32[1,512,512]{1,2,0:T(8,128)}, u32[]{:S(2)}) copy-start(f32[1,512,512]{1,2,0:T(8,128)} %all-reduce.7.cloned.1.call-done) | copy-start | bytes 3145732
  324.5 0.7 copy-start.8
  361.5 1.9 copy-start.6
Sparse Core Ops, SparseCore 0:
  11.3 30.4 all-gather.4
  43.4 72.8 all-gather.2
  269.2 51.1 all-reduce.6
Sparse Core Ops, SparseCore 1:
  14.4 112.6 all-reduce.4
  129.3 75.8 reduce-scatter.1
where the time goes:
time: 410 us; the launch traced here: 401 us
  other arithmetic  169 us (41%)
  waiting for transfers between devices  155 us (38%)
  matrix products  40 us (10%)
  local copies, waits for them, and re-layouts  20.5 us (5%)
  between operations  17.1 us (4%)
    another operation x16, other arithmetic, eliminate(): factor = jnp.linalg.cholesky(dense[:redundant, :redundant])  102 us
    psum x1, waiting for transfers between devices, per_device(): summed = lax.psum(partial_value, 'col')  75.6 us
    another operation x6, other arithmetic, eliminate(): jax.scipy.linalg.cho_solve((factor, True), dense[:redundant, redundant:])  61.1 us
    psum x1, waiting for transfers between devices, per_device(): parent_dense = lax.psum(parent_part, 'col')  51.3 us
    all_gather x1, waiting for transfers between devices, per_device(): lax.all_gather(cluster_bases[:, :, redundant:], 'row', axis=0, tiled=True)  26.7 us
    another operation x12, local copies, waits for them, and re-layouts  9.11 us
  transfers between devices with their start and end apart: 6, of which 4 were waited for; matrix products, arithmetic and copies ran while one was open for 36% of the time, Pallas kernels for 0%

commit v1 on v0

--- a/solution.py
+++ b/solution.py
@@ -30,7 +30,10 @@
     own_rows = cluster_bases.shape[1]
     full_bases = lax.all_gather(cluster_bases, "col", axis=1, tiled=True)
     partial_value = jnp.einsum("cij,cjk->cik", diag_blocks, cluster_bases, precision=highest)
-    summed = lax.psum(partial_value, "col")
+    size, summed = (lax.axis_size("col"), partial_value)
+    for far in [1 << k for k in range(size.bit_length() - 1)]:
+        pairs = [(i_2, i_2 ^ far) for i_2 in range(size)]
+        summed = summed + lax.ppermute(summed, "col", pairs)
     dense = jnp.einsum("cji,cjk->cik", full_bases, summed, precision=highest)
     solved, schur = jax.vmap(lambda single: eliminate(single, redundant))(dense)
     leaf_diag = lax.dynamic_slice_in_dim(schur, column * quarter, quarter, 2)

time: 410 us -> 536 us (1.31)
  waiting for transfers between devices: 155 us -> 272 us
  starting transfers between devices: 0.28 us -> 8.71 us
    ppermute x0 -> x2, waiting for transfers between devices: none -> 194 us  [per_device(): summed = summed + lax.ppermute(summed, 'col', pairs)]
    psum x1 -> x0, waiting for transfers between devices: 75.6 us -> none  [per_device(): summed = lax.psum(partial_value, 'col')]
    ppermute x0 -> x2, starting transfers between devices: none -> 8.18 us  [per_device(): summed = summed + lax.ppermute(summed, 'col', pairs)]
  transfers between devices with their start and end apart: 6 -> 7, of which waited for: 4 -> 6; matrix products, arithmetic and copies ran while one was open for 36% -> 28% of each run, Pallas kernels for 0% -> 0%
where the time goes in v1:
time: 536 us; the launch traced here: 531 us
  waiting for transfers between devices  272 us (51%)
  other arithmetic  174 us (32%)
  matrix products  39.6 us (7%)
  local copies, waits for them, and re-layouts  20.4 us (4%)
  between operations  15.7 us (3%)
  starting transfers between devices  8.71 us (2%)
    ppermute x2, waiting for transfers between devices, per_device(): summed = summed + lax.ppermute(summed, 'col', pairs)  194 us
    another operation x16, other arithmetic, eliminate(): factor = jnp.linalg.cholesky(dense[:redundant, :redundant])  103 us
    another operation x6, other arithmetic, eliminate(): jax.scipy.linalg.cho_solve((factor, True), dense[:redundant, redundant:])  61.9 us
    psum x1, waiting for transfers between devices, per_device(): parent_dense = lax.psum(parent_part, 'col')  53 us
    all_gather x1, waiting for transfers between devices, per_device(): lax.all_gather(cluster_bases[:, :, redundant:], 'row', axis=0, tiled=True)  23.7 us
  transfers between devices with their start and end apart: 7, of which 6 were waited for; matrix products, arithmetic and copies ran while one was open for 28% of the time, Pallas kernels for 0%

profile of v1, /device:TPU:0, one launch (start us, length us, event | category | flops | bytes accessed | tf_op | source)
XLA Modules:
  0.0 530.8 jit_solution(7468563825464074832)
XLA Ops:
  7.2 1.8 slice.175
  9.9 4.4 fusion.66
  14.2 3.1 collective-permute-start
  17.3 23.7 %all-gather.5.cloned.1.call-done = f32[16,128,256]{2,1,0:T(8,128)} async-done(((f32[2,128,256]{2,1,0:T(8,128)}), f32[16,128,256]{2,1,0:T(8,128)}) %all-gather.5.cloned.1.call-update) | async-done | bytes 2097168 | tf_op jit(solution)/shard_map/all_gather | solution.py:41
  41.0 3.8 fusion
  44.8 5.1 convolution_bitcast_fusion
  50.3 39.1 %collective-permute-done = f32[2,512,512]{2,1,0:T(8,128)} collective-permute-done((f32[2,512,512]{2,1,0:T(8,128)}, f32[2,512,512]{2,1,0:T(8,128)}, u32[]{:S(2)}, u32[]{:S(2)}) %collective-permute-start) | collective-permute-done | bytes 2097184 | tf_op jit(solution)/shard_map/ppermute | solution.py:36
  89.4 4.1 add.86
  93.5 5.1 collective-permute-start.1
  99.5 154.4 %collective-permute-done.1 = f32[2,512,512]{2,1,0:T(8,128)} collective-permute-done((f32[2,512,512]{2,1,0:T(8,128)}, f32[2,512,512]{2,1,0:T(8,128)}, u32[]{:S(2)}, u32[]{:S(2)}) %collective-permute-start.1) | collective-permute-done | bytes 2097184 | tf_op jit(solution)/shard_map/ppermute | solution.py:36
  253.9 6.2 %fusion.6 = f32[2,512,512]{1,2,0:T(8,128)S(1)} fusion(f32[2,512,512]{2,1,0:T(8,128)} %all-gather.3.cloned.1.call-done, f32[2,512,512]{2,1,0:T(8,128)} %add.86, f32[2,512,512]{2,1,0:T(8,128)} %collective-permute-done.1), kind=kOutput, calls=%fused_computation.12 | convolution fusion | flops 3221749760 | bytes 8388608 | tf_op jit(solution)/shard_map/cji,cjk->cik/dot_general | solution.py:37
  263.7 23.5 %custom-call.40 = f32[2,128,128]{2,1,0:T(8,128)S(1)} custom-call(f32[2,128,128]{2,1,0:T(8,128)S(1)} %cholesky.239), custom_call_target="Cholesky" | custom-call | tf_op jit(solution)/shard_map/vmap(jit(cholesky))/cholesky | solution.py:17
  287.2 20.3 %custom-call.41 = f32[2,1,128,128]{2,3,1,0:T(8,128)} custom-call(f32[2,1,128,128]{3,2,1,0:T(8,128)S(1)} %select_bitcast_fusion), custom_call_target="InvertDiagBlocksLowerTriangular" | custom-call | tf_op jit(solution)/shard_map/vmap(jit(cholesky))/cholesky | solution.py:17
  309.1 24.0 %custom-call.42 = f32[2,128,128]{2,1,0:T(8,128)S(1)} custom-call(f32[2,128,128]{2,1,0:T(8,128)S(1)} %convolution_subtract_fusion.2), custom_call_target="Cholesky" | custom-call | tf_op jit(solution)/shard_map/vmap(jit(cholesky))/cholesky | solution.py:17
  333.5 5.1 while.2
  334.1 2.0 bitcast_dynamic-update-slice_fusion.5
  336.7 2.0 bitcast_dynamic-update-slice_fusion.5
  338.7 40.3 %custom-call.43 = f32[2,2,128,128]{2,3,1,0:T(8,128)S(1)} custom-call(f32[2,2,128,128]{3,2,1,0:T(8,128)} %bitcast.190), custom_call_target="InvertDiagBlocksLowerTriangular" | custom-call | tf_op jit(solution)/shard_map/vmap(jit(_cho_solve))/triangular_solve | solution.py:18
  380.9 1.4 fusion.25
  383.5 2.1 fusion.21
  386.6 3.9 fusion.9
  395.2 2.0 convolution_bitcast_fusion.1
  397.3 53.0 %all-reduce.4.cloned.1.call-done = f32[1,512,512]{1,2,0:T(8,128)} async-done(((f32[1,512,512]{1,2,0:T(8,128)}), f32[1,512,512]{1,2,0:T(8,128)}) %all-reduce.4.cloned.1.call-update) | async-done | bytes 1048592 | tf_op jit(solution)/shard_map/psum | solution.py:72
  450.3 1.9 fusion.65
  455.1 11.7 %custom-call.44 = f32[1,128,128]{2,1,0:T(8,128)S(1)} custom-call(f32[1,128,128]{2,1,0:T(8,128)S(1)} %cholesky.242), custom_call_target="Cholesky" | custom-call | tf_op jit(solution)/shard_map/vmap(jit(cholesky))/cholesky | solution.py:17
  466.8 10.0 %custom-call.45 = f32[1,1,128,128]{2,3,1,0:T(8,128)S(1)} custom-call(f32[1,1,128,128]{3,2,1,0:T(8,128)S(1)} %get-tuple-element.57), custom_call_target="InvertDiagBlocksLowerTriangular" | custom-call | tf_op jit(solution)/shard_map/vmap(jit(cholesky))/cholesky | solution.py:17
  479.0 11.7 %custom-call.46 = f32[1,128,128]{2,1,0:T(8,128)S(1)} custom-call(f32[1,128,128]{2,1,0:T(8,128)S(1)} %fusion.16), custom_call_target="Cholesky" | custom-call | tf_op jit(solution)/shard_map/vmap(jit(cholesky))/cholesky | solution.py:17
  494.3 5.3 while.3
  495.0 2.0 bitcast_dynamic-update-slice_fusion.6
  497.6 2.0 bitcast_dynamic-update-slice_fusion.6
  499.6 20.5 %custom-call.47 = f32[1,2,128,128]{2,3,1,0:T(8,128)S(1)} custom-call(f32[1,2,128,128]{3,2,1,0:T(8,128)} %bitcast.191), custom_call_target="InvertDiagBlocksLowerTriangular" | custom-call | tf_op jit(solution)/shard_map/vmap(jit(_cho_solve))/triangular_solve | solution.py:18
  522.6 1.5 dynamic-slice_subtract_fusion.1
  (92 shorter events, 28.7 us)
Async XLA Ops:
  7.2 37.7 %copy-start = (f32[2,4,512,128]{3,2,1,0:T(8,128)S(1)}, f32[2,4,512,128]{3,2,1,0:T(8,128)}, u32[]{:S(2)}) copy-start(f32[2,4,512,128]{3,2,1,0:T(8,128)} %param.7) | copy-start | bytes 6291460
  7.2 33.8 %all-gather.5.cloned.1.call-start = ((), (), s32[]{:S(2)}) async-start(), calls=%async_computation.2 | async-start | bytes 2359296 | tf_op jit(solution)/shard_map/all_gather | solution.py:41
  9.0 31.9 %copy-start.8 = (s32[2,4]{1,0:T(2,128)S(1)}, s32[2,4]{1,0:T(2,128)}, u32[]{:S(2)}) copy-start(s32[2,4]{1,0:T(2,128)} %param.9) | copy-start | bytes 100
  9.1 90.4 %all-gather.3.cloned.1.call-start = ((), (), s32[]{:S(2)}) async-start(), calls=%async_computation.1 | async-start | bytes 2621440 | tf_op jit(solution)/shard_map/all_gather | solution.py:31
  9.8 376.8 %reduce-scatter.2.cloned.1.call-start = ((), (), s32[]{:S(2)}) async-start(), calls=%async_computation.3 | async-start | bytes 5242880 | tf_op jit(solution)/shard_map/reduce_scatter | solution.py:49
  14.2 75.2 %collective-permute-start = (f32[2,512,512]{2,1,0:T(8,128)}, f32[2,512,512]{2,1,0:T(8,128)}, u32[]{:S(2)}, u32[]{:S(2)}) collective-permute-start(f32[2,512,512]{2,1,0:T(8,128)} %fusion.66), channel_id=1, source_target_pairs={{0,1},{1,0},{2,3},{3,2},{4,5},{5,4},{6,7},{7,6},{8,9},{9,8},{10,11... | collective-permute-start | bytes 6291464 | tf_op jit(solution)/shard_map/ppermute | solution.py:36
  50.0 48.8 %copy-start.9 = (s32[2]{0:T(128)S(1)}, s32[2]{0:T(128)}, u32[]{:S(2)}) copy-start(s32[2]{0:T(128)} %param.10) | copy-start | bytes 28
  50.0 400.3 %all-reduce.4.cloned.1.call-start = ((), (), s32[]{:S(2)}) async-start(), calls=%async_computation.4 | async-start | bytes 2097152 | tf_op jit(solution)/shard_map/psum | solution.py:72
  93.5 160.4 %collective-permute-start.1 = (f32[2,512,512]{2,1,0:T(8,128)}, f32[2,512,512]{2,1,0:T(8,128)}, u32[]{:S(2)}, u32[]{:S(2)}) collective-permute-start(f32[2,512,512]{2,1,0:T(8,128)} %add.86), channel_id=1, source_target_pairs={{0,2},{1,3},{2,0},{3,1},{4,6},{5,7},{6,4},{7,5},{8,10},{9,11},{10,... | collective-permute-start | bytes 6291464 | tf_op jit(solution)/shard_map/ppermute | solution.py:36
  260.1 1.3 copy-start.1
  386.6 7.0 %copy-start.4 = (f32[2,256,64]{1,2,0:T(8,128)}, f32[2,256,64]{1,2,0:T(8,128)S(1)}, u32[]{:S(2)}) copy-start(f32[2,256,64]{1,2,0:T(8,128)S(1)} %dynamic-slice_subtract_fusion) | copy-start | bytes 393220
  391.2 0.8 copy-start.6
  392.0 2.6 copy-start.3
  392.0 1.5 collective-permute-start.2
  452.2 67.9 %copy-start.2 = (f32[1,512,512]{1,2,0:T(8,128)S(1)}, f32[1,512,512]{1,2,0:T(8,128)}, u32[]{:S(2)}) copy-start(f32[1,512,512]{1,2,0:T(8,128)} %all-reduce.4.cloned.1.call-done) | copy-start | bytes 3145732
  454.4 0.7 copy-start.7
  491.4 1.9 copy-start.5
Sparse Core Ops, SparseCore 0:
  10.4 30.4 all-gather.4
  42.6 56.8 all-gather.2
  101.8 130.0 reduce-scatter.1
  397.4 52.8 all-reduce.3
